TPU v7x, 32 devices: a whole 2x2x4 slice. The times are simulated.
32 devices in a mesh: req: 8 (over y, x, core), cand: 4 (over z).
Axes of the slice: x: 2, y: 2, z: 4, core: 2. Of those that a mesh axis runs over, the one named last changes fastest.
Arguments:
- history: bfloat16 [64, 256, 1024], P('req', 'cand'), may hold values from -6 to 6
- history_length: int32 [64], P('req'), may hold values from 32 to 256
- candidate_count: int32 [64], P('req'), may hold values from 512 to 4096
- block_shard: int32 [64, 32], P('req'), may hold values from 0 to 3, as said below
- block_index: int32 [64, 32], P('req'), may hold values from 0 to 3
- item_table: bfloat16 [16, 128, 1024], P('cand'), may hold values from -6 to 6
- item_ages: int32 [64, 4096], P('req', 'cand'), may hold values from 0 to 336
- history_weight: bfloat16 [1024, 2048], P('req'), may hold values from -0.1875 to 0.1875
- candidate_weight: bfloat16 [1024, 2048], P('req'), may hold values from -0.1875 to 0.1875
- output_weight: bfloat16 [1024, 1024], P('req'), may hold values from -0.1875 to 0.1875
- hidden_weight: bfloat16 [1024, 256], P('req'), may hold values from -0.1875 to 0.1875
- norm_gain: float32 [1024], replicated, may hold values from 0.1 to 1.9
- score_weight: bfloat16 [2, 256], replicated, may hold values from -0.375 to 0.375
Outputs:
- scores: float32 [64, 4096], P('req', 'cand')
Inputs may be any that keep to these rules, and one draw needn't show every extreme that they name: `block_shard`: for each group of 8 consecutive requests (aligned) and each c, the slots j with j // 8 == c of those requests name every shard exactly 16 times.
All inputs are finite; a program needn't handle non-finite values.
Results may differ from a plain program's by a relative error of at most 0.0053.
Values may be sent and summed in bfloat16 or wider, within the bound.
A program may use at most 128 MiB of HBM per device.

v0:
```python
import math
import jax
import jax.numpy as jnp
from jax import lax
from jax.sharding import PartitionSpec as P

HEADS = 8
BLOCK = 128
EPSILON = 1e-05
AGE_SCALE = 48.0


def local(
    history,
    history_length,
    candidate_count,
    block_shard,
    block_index,
    item_table,
    item_ages,
    history_weight,
    candidate_weight,
    output_weight,
    hidden_weight,
    norm_gain,
    score_weight,
):
    proj_history, proj_candidate, proj_output, proj_hidden = (
        lax.all_gather(history_weight, "req", axis=0, tiled=True),
        lax.all_gather(candidate_weight, "req", axis=0, tiled=True),
        lax.all_gather(output_weight, "req", axis=0, tiled=True),
        lax.all_gather(hidden_weight, "req", axis=0, tiled=True),
    )
    shards = lax.axis_size("cand")
    my_shard = lax.axis_index("cand")
    requests, max_blocks = block_shard.shape
    per_scorer = max_blocks // shards
    slot_count = requests * per_scorer
    capacity = slot_count // shards
    model_width = item_table.shape[2]
    head_size = model_width // HEADS
    score_scale = 1.0 / math.sqrt(head_size)
    shard_sets = (
        block_shard.reshape(requests, shards, per_scorer)
        .transpose(1, 0, 2)
        .reshape(shards, slot_count)
    )
    index_sets = (
        block_index.reshape(requests, shards, per_scorer)
        .transpose(1, 0, 2)
        .reshape(shards, slot_count)
    )
    is_mine = (shard_sets == my_shard).astype(jnp.int32)
    before = jnp.cumsum(is_mine, axis=1) - is_mine
    picked = is_mine[:, None, :] * (
        before[:, None, :] == jnp.arange(capacity, dtype=jnp.int32)[None, :, None]
    ).astype(jnp.int32)
    send_ids = jnp.sum(picked * index_sets[:, None, :], axis=2)
    outgoing = item_table[send_ids]
    incoming = lax.all_to_all(outgoing, "cand", split_axis=0, concat_axis=0, tiled=True)
    own_shard = lax.dynamic_index_in_dim(shard_sets, my_shard, 0, keepdims=False)
    matches = (own_shard[:, None] == jnp.arange(shards, dtype=jnp.int32)[None, :]).astype(jnp.int32)
    own_rank = jnp.sum((jnp.cumsum(matches, axis=0) - matches) * matches, axis=1)
    arrived = incoming.reshape(shards * capacity, BLOCK, model_width)[
        own_shard * capacity + own_rank
    ]
    arrived = arrived.reshape(requests, per_scorer, BLOCK, model_width)
    first_block = jnp.zeros((requests,), jnp.int32) + my_shard * per_scorer
    block_number = first_block[:, None] + jnp.arange(per_scorer, dtype=jnp.int32)[None, :]
    live_slots = (block_number * BLOCK < candidate_count[:, None]).reshape(slot_count)
    request_of = jnp.arange(slot_count, dtype=jnp.int32) // per_scorer
    local_pairs = jax.nn.silu(
        jnp.dot(history.reshape(-1, model_width), proj_history, preferred_element_type=jnp.float32)
    ).astype(jnp.bfloat16)
    local_pairs = local_pairs.reshape(requests, -1, 2 * model_width)
    projected = lax.all_gather(local_pairs, "cand", axis=1, tiled=True)
    history_total = projected.shape[1]
    positions = jnp.arange(history_total, dtype=jnp.int32)
    query_weight = proj_candidate[:, :model_width]
    gate_weight = proj_candidate[:, model_width:]

    def score_slot(operands):
        block_rows, request, is_live = operands

        def score_block(block_rows):
            query = jax.nn.silu(
                jnp.dot(block_rows, query_weight, preferred_element_type=jnp.float32)
            ).astype(jnp.bfloat16)
            query = query.reshape(BLOCK, HEADS, head_size)
            pair_rows = lax.dynamic_index_in_dim(projected, request, 0, keepdims=False)
            key_rows = pair_rows[:, :model_width].reshape(history_total, HEADS, head_size)
            value_rows = pair_rows[:, model_width:].reshape(history_total, HEADS, head_size)
            length = lax.dynamic_index_in_dim(history_length, request, 0, keepdims=False)
            scores = (
                jnp.einsum("ihd,phd->hip", query, key_rows, preferred_element_type=jnp.float32)
                * score_scale
            )
            weights = jax.nn.silu(scores) / length.astype(jnp.float32)
            weights = jnp.where(positions[None, None, :] < length, weights, 0.0).astype(
                jnp.bfloat16
            )
            attended = jnp.einsum(
                "hip,phd->ihd", weights, value_rows, preferred_element_type=jnp.float32
            ).reshape(BLOCK, model_width)
            gate = jax.nn.silu(jnp.dot(block_rows, gate_weight, preferred_element_type=jnp.float32))
            center = attended - jnp.mean(attended, axis=-1, keepdims=True)
            spread = jnp.mean(center * center, axis=-1, keepdims=True)
            normed = (center * lax.rsqrt(spread + EPSILON) * norm_gain * gate).astype(jnp.bfloat16)
            merged = (
                jnp.dot(normed, proj_output, preferred_element_type=jnp.float32)
                + block_rows.astype(jnp.float32)
            ).astype(jnp.bfloat16)
            hidden = jax.nn.silu(
                jnp.dot(merged, proj_hidden, preferred_element_type=jnp.float32)
            ).astype(jnp.bfloat16)
            return jnp.einsum("ik,ck->ci", hidden, score_weight, preferred_element_type=jnp.float32)

        def empty_block(block_rows):
            return jnp.zeros((2, BLOCK), jnp.float32)

        return lax.cond(is_live, score_block, empty_block, block_rows)

    logits = lax.map(
        score_slot, (arrived.reshape(slot_count, BLOCK, model_width), request_of, live_slots)
    )
    logits = logits.reshape(requests, per_scorer, 2, BLOCK)
    decays = jnp.exp(
        -item_ages.astype(jnp.float32).reshape(requests, per_scorer, BLOCK) / AGE_SCALE
    )
    blended = decays * logits[:, :, 0] + (1.0 - decays) * logits[:, :, 1]
    row_number = (my_shard * per_scorer + jnp.arange(per_scorer, dtype=jnp.int32))[
        None, :, None
    ] * BLOCK + jnp.arange(BLOCK, dtype=jnp.int32)[None, None, :]
    kept_rows = row_number < candidate_count[:, None, None]
    return jnp.where(kept_rows, blended, 0.0).reshape(requests, per_scorer * BLOCK)


def solution(mesh):
    return jax.shard_map(
        local,
        mesh=mesh,
        in_specs=(
            P("req", "cand", None),
            P("req"),
            P("req"),
            P("req", None),
            P("req", None),
            P("cand", None, None),
            P("req", "cand"),
            P("req", None),
            P("req", None),
            P("req", None),
            P("req", None),
            P(),
            P(),
        ),
        out_specs=P("req", "cand"),
        check_vma=False,
    )
```

profile of v0, /device:TPU:3, one launch (start us, length us, event | category | flops | bytes accessed | tf_op | source)
XLA Modules:
  0.0 1650.8 jit_solution(6157410167003567485)
XLA Ops:
  25.0 22.5 %all-gather.5.cloned.1.call-done = bf16[1024,2048]{1,0:T(8,128)(2,1)} async-done(((bf16[128,2048]{1,0:T(8,128)(2,1)}), bf16[1024,2048]{1,0:T(8,128)(2,1)}) %all-gather.5.cloned.1.call-update) | async-done | bytes 4194320 | tf_op jit(solution)/shard_map/all_gather | solution.py:29
  68.9 19.3 %all-gather.9.cloned.1.call-done = bf16[1024,2048]{1,0:T(8,128)(2,1)} async-done(((bf16[128,2048]{1,0:T(8,128)(2,1)}), bf16[1024,2048]{1,0:T(8,128)(2,1)}) %all-gather.9.cloned.1.call-update) | async-done | bytes 4194320 | tf_op jit(solution)/shard_map/all_gather | solution.py:30
  92.3 277.3 %all-gather.7.cloned.1.call-done = bf16[8,256,2048]{2,0,1:T(8,128)(2,1)} async-done(((bf16[8,64,2048]{2,0,1:T(8,128)(2,1)}), bf16[8,256,2048]{2,0,1:T(8,128)(2,1)}) %all-gather.7.cloned.1.call-update) | async-done | bytes 8388624 | tf_op jit(solution)/shard_map/all_gather | solution.py:76
  382.2 139.2 %all-to-all-done = bf16[4,16,128,1024]{3,2,1,0:T(8,128)(2,1)} async-done(((bf16[4,16,128,1024]{3,2,1,0:T(8,128)(2,1)}), bf16[4,16,128,1024]{3,2,1,0:T(8,128)(2,1)}, u32[]{:S(2)}, u32[]{:S(2)}) %all-to-all-start) | async-done | bytes 16777248 | tf_op jit(solution)/shard_map/all_to_all | solution.py:60
  534.9 1108.1 %while.11 = (s32[]{:T(128)}, f32[64,2,128]{2,1,0:T(2,128)S(1)}, pred[64]{0:T(512)(128)(4,1)S(1)}, bf16[8,256,2048]{1,2,0:T(8,128)(2,1)}, s32[8]{0:T(128)S(1)}, /...) while((s32[]{:T(128)}, f32[64,2,128]{2,1,0:T(2,128)S(1)}, ...), condition=%wide.region_9.10_spmd.clone, body=%wide.region_4.9_spmd.clone.sunk | while | flops 1011778432 | bytes 19286676 | solution.py:123
  536.3 16.0 conditional.3
  553.6 15.9 conditional.3
  570.9 15.9 conditional.3
  588.2 15.9 conditional.3
  605.6 15.9 conditional.3
  622.9 15.9 conditional.3
  640.2 15.9 conditional.3
  657.5 15.9 conditional.3
  674.8 15.9 conditional.3
  692.1 15.9 conditional.3
  709.4 15.9 conditional.3
  726.8 15.9 conditional.3
  744.1 15.9 conditional.3
  761.4 15.9 conditional.3
  778.7 15.9 conditional.3
  796.0 15.9 conditional.3
  813.3 15.9 conditional.3
  830.6 15.9 conditional.3
  848.0 15.9 conditional.3
  865.3 15.9 conditional.3
  882.6 15.9 conditional.3
  899.9 15.9 conditional.3
  917.2 15.9 conditional.3
  934.5 15.9 conditional.3
  951.8 15.9 conditional.3
  1280.8 15.9 conditional.3
  1609.8 15.9 conditional.3
  (1507 shorter events, 1555.9 us)
Async XLA Ops:
  6.5 40.9 %all-gather.5.cloned.1.call-start = ((), (), s32[]{:S(2)}) async-start(), calls=%async_computation.1 | async-start | bytes 4718592 | tf_op jit(solution)/shard_map/all_gather | solution.py:29
  17.0 30.5 %copy-start.7 = (bf16[8,64,1024]{2,1,0:T(8,128)(2,1)S(1)}, bf16[8,64,1024]{2,1,0:T(8,128)(2,1)}, u32[]{:S(2)}) copy-start(bf16[8,64,1024]{2,1,0:T(8,128)(2,1)} %param.17) | copy-start | bytes 3145732
  17.0 504.5 %all-to-all-start = ((bf16[4,16,128,1024]{3,2,1,0:T(8,128)(2,1)}), bf16[4,16,128,1024]{3,2,1,0:T(8,128)(2,1)}, u32[]{:S(2)}, u32[]{:S(2)}) async-start(bf16[4,16,128,1024]{3,2,1,0:T(8,128)(2,1)} %bitcast.105), calls=%async_computation | async-start | bytes 33554432 | tf_op jit(solution)/shard_map/all_to_all | solution.py:60
  24.2 64.0 %all-gather.9.cloned.1.call-start = ((), (), s32[]{:S(2)}) async-start(), calls=%async_computation.3 | async-start | bytes 4718592 | tf_op jit(solution)/shard_map/all_gather | solution.py:30
  25.0 344.6 %all-gather.7.cloned.1.call-start = ((), (), s32[]{:S(2)}) async-start(), calls=%async_computation.2 | async-start | bytes 10485760 | tf_op jit(solution)/shard_map/all_gather | solution.py:76
  55.0 479.9 %all-gather.11.cloned.1.call-start = ((), (), s32[]{:S(2)}) async-start(), calls=%async_computation.4 | async-start | bytes 2359296 | tf_op jit(solution)/shard_map/all_gather | solution.py:31
  521.4 13.5 copy-start.5
  521.5 13.5 copy-start.8
  521.5 13.5 copy-start.9
  534.9 1108.2 %copy-start.4 = (s32[8,1024]{1,0:T(8,128)S(1)}, s32[8,1024]{1,0:T(8,128)}, u32[]{:S(2)}) copy-start(s32[8,1024]{1,0:T(8,128)} %param.23) | copy-start | bytes 98308
  576.0 4.6 copy-start.2
  593.3 4.6 copy-start.2
  662.6 4.6 copy-start.2
  679.9 4.6 copy-start.2
  749.1 4.6 copy-start.2
  766.4 4.6 copy-start.2
  835.7 4.6 copy-start.2
  853.0 4.6 copy-start.2
  904.9 4.6 copy-start.2
  922.3 4.6 copy-start.2
  991.5 4.6 copy-start.2
  1008.8 4.6 copy-start.2
  1078.1 4.6 copy-start.2
  1095.4 4.6 copy-start.2
  1164.7 4.6 copy-start.2
  1182.0 4.6 copy-start.2
  1233.9 4.6 copy-start.2
  1251.2 4.6 copy-start.2
  1320.5 4.6 copy-start.2
  1337.8 4.6 copy-start.2
  1407.0 4.6 copy-start.2
  1424.4 4.6 copy-start.2
  (46 other events, 204.7 us)
Sparse Core Ops, SparseCore 0:
  9.2 38.2 all-gather.4
  49.4 38.7 all-gather.8
  89.8 279.6 all-gather.6
  371.3 143.0 all-gather.10
where the time goes:
time: 1670 us; the launch traced here: 1650 us
  matrix products  567 us (34%)
  waiting for transfers between devices  460 us (28%)
  local copies, waits for them, and re-layouts  328 us (20%)
  loops' own time  214 us (13%)
  other arithmetic  48.9 us (3%)
    all_gather x1, waiting for transfers between devices, local(): projected = lax.all_gather(local_pairs, 'cand', axis=1, tiled=True)  277 us
    dot_general x64, matrix products, score_block(): jnp.dot(block_rows, query_weight, preferred_element_type=jnp.float32)  185 us
    another operation x64, loops' own time, score_slot(): return lax.cond(is_live, score_block, empty_block, block_rows)  169 us
    dot_general x64, matrix products, score_block(): jnp.dot(merged, proj_hidden, preferred_element_type=jnp.float32)  164 us
    all_to_all x1, waiting for transfers between devices, local(): lax.all_to_all(outgoing, 'cand', split_axis=0, concat_axis=0, tiled=True)  139 us
    dot_general x64, matrix products, score_block(): jnp.einsum('hip,phd->ihd', weights, value_rows, preferred_element_type=jn...  116 us
    dot_general x64, matrix products, score_block(): jnp.dot(block_rows, gate_weight, preferred_element_type=jnp.float32)  89.4 us
    dynamic_slice x128, local copies, waits for them, and re-layouts, local(): lax.map(score_slot, (arrived.reshape(slot_count, BLOCK, model_width), req...  83.3 us
  transfers between devices with their start and end apart: 5, of which 4 were waited for; matrix products, arithmetic and copies ran while one was open for 3% of the time, Pallas kernels for 0%

commit v1 on v0

--- a/solution.py
+++ b/solution.py
@@ -8,6 +8,12 @@
 BLOCK = 128
 EPSILON = 1e-05
 AGE_SCALE = 48.0
+
+
+def in_order(blocks, dim):
+    blocks = jnp.moveaxis(blocks, 0, dim)
+    lengths = blocks.shape
+    return blocks.reshape(*lengths[:dim], lengths[dim] * lengths[dim + 1], *lengths[dim + 2 :])
 
 
 def local(
@@ -73,7 +79,19 @@
         jnp.dot(history.reshape(-1, model_width), proj_history, preferred_element_type=jnp.float32)
     ).astype(jnp.bfloat16)
     local_pairs = local_pairs.reshape(requests, -1, 2 * model_width)
-    projected = lax.all_gather(local_pairs, "cand", axis=1, tiled=True)
+    size = lax.axis_size("cand")
+    pairs = [(i, (i + 1) % size) for i in range(size)]
+    back = [(b, a) for a, b in pairs]
+    lower, upper = ([], [])
+    for step in range(size - 1):
+        if step % 2 == 0:
+            lower.append(lax.ppermute(lower[-1] if lower else local_pairs, "cand", pairs))
+        else:
+            upper.append(lax.ppermute(upper[-1] if upper else local_pairs, "cand", back))
+    blocks = jnp.stack([*lower[::-1], local_pairs, *upper])
+    shift = lax.axis_index("cand") - len(lower)
+    blocks = blocks[(jnp.arange(size) - shift) % size]
+    projected = in_order(blocks, 1)
     history_total = projected.shape[1]
     positions = jnp.arange(history_total, dtype=jnp.int32)
     query_weight = proj_candidate[:, :model_width]

time: 1670 us -> 1700 us (1.018)
  starting transfers between devices: 7.37 us -> 143 us
  waiting for transfers between devices: 460 us -> 334 us
    ppermute x0 -> x3, waiting for transfers between devices: none -> 293 us  [the longest x2 293 us: local(): lax.ppermute(lower[-1] if lower else local_pairs, 'cand', pairs)]
    all_gather x1 -> x0, waiting for transfers between devices: 277 us -> none  [local(): projected = lax.all_gather(local_pairs, 'cand', axis=1, tiled=True)]
    all_to_all x1, waiting for transfers between devices: 139 us -> 0.01 us  [local(): lax.all_to_all(outgoing, 'cand', split_axis=0, concat_axis=0, tiled=True)]
    ppermute x0 -> x3, starting transfers between devices: none -> 135 us  [the longest x2 133 us: local(): lax.ppermute(lower[-1] if lower else local_pairs, 'cand', pairs)]
    all_gather x1, waiting for transfers between devices: 19.3 us -> 0.01 us  [local(): lax.all_gather(candidate_weight, 'req', axis=0, tiled=True)]
    all_gather x1, waiting for transfers between devices: 22.5 us -> 39.6 us  [local(): lax.all_gather(history_weight, 'req', axis=0, tiled=True)]
  transfers between devices with their start and end apart: 5 -> 7, of which waited for: 4 -> 3; matrix products, arithmetic and copies ran while one was open for 3% -> 4% of each run, Pallas kernels for 0% -> 0%
where the time goes in v1:
time: 1700 us; the launch traced here: 1680 us
  matrix products  569 us (33%)
  local copies, waits for them, and re-layouts  344 us (20%)
  waiting for transfers between devices  334 us (20%)
  loops' own time  201 us (12%)
  starting transfers between devices  143 us (8%)
  other arithmetic  65.4 us (4%)
    ppermute x2, waiting for transfers between devices, local(): lax.ppermute(lower[-1] if lower else local_pairs, 'cand', pairs)  293 us
    dot_general x64, matrix products, score_block(): jnp.dot(block_rows, query_weight, preferred_element_type=jnp.float32)  185 us
    dot_general x64, matrix products, score_block(): jnp.dot(merged, proj_hidden, preferred_element_type=jnp.float32)  163 us
    another operation x64, loops' own time, score_slot(): return lax.cond(is_live, score_block, empty_block, block_rows)  161 us
    ppermute x2, starting transfers between devices, local(): lax.ppermute(lower[-1] if lower else local_pairs, 'cand', pairs)  133 us
    dot_general x64, matrix products, score_block(): jnp.einsum('hip,phd->ihd', weights, value_rows, preferred_element_type=jn...  116 us
    dot_general x64, matrix products, score_block(): jnp.dot(block_rows, gate_weight, preferred_element_type=jnp.float32)  89.4 us
    squeeze x64, local copies, waits for them, and re-layouts, score_block(): pair_rows = lax.dynamic_index_in_dim(projected, request, 0, keepdims=False)  83.2 us
  transfers between devices with their start and end apart: 7, of which 3 were waited for; matrix products, arithmetic and copies ran while one was open for 4% of the time, Pallas kernels for 0%

profile of v1, /device:TPU:3, one launch (start us, length us, event | category | flops | bytes accessed | tf_op | source)
XLA Modules:
  0.0 1682.0 jit_solution(1806199480560366053)
XLA Ops:
  25.0 39.6 %all-gather.4.cloned.1.call-done = bf16[1024,2048]{1,0:T(8,128)(2,1)} async-done(((bf16[128,2048]{1,0:T(8,128)(2,1)}), bf16[1024,2048]{1,0:T(8,128)(2,1)}) %all-gather.4.cloned.1.call-update) | async-done | bytes 4194320 | tf_op jit(solution)/shard_map/all_gather | solution.py:35
  74.2 267.6 %collective-permute-done = bf16[8,64,2048]{2,1,0:T(8,128)(2,1)} collective-permute-done((bf16[8,64,2048]{2,1,0:T(8,128)(2,1)}, bf16[8,64,2048]{2,1,0:T(8,128)(2,1)}, u32[]{:S(2)}, u32[]{:S(2)}) %collective-permute-start) | collective-permute-done | bytes 2097184 | tf_op jit(solution)/shard_map/ppermute | solution.py:88
  341.8 132.2 %collective-permute-start.1 = (bf16[8,64,2048]{2,1,0:T(8,128)(2,1)}, bf16[8,64,2048]{2,1,0:T(8,128)(2,1)}, u32[]{:S(2)}, u32[]{:S(2)}) collective-permute-start(bf16[8,64,2048]{2,1,0:T(8,128)(2,1)} %collective-permute-done), channel_id=1, source_target_pairs={{0,1},{1,2},{2,3},{3,0},{4,5},{5,6},{6,7},{7,4},{8,9},{9,10},{10,1... | collective-permute-start | bytes 6291464 | tf_op jit(solution)/shard_map/ppermute | solution.py:88
  492.6 25.2 %collective-permute-done.1 = bf16[8,64,2048]{2,1,0:T(8,128)(2,1)} collective-permute-done((bf16[8,64,2048]{2,1,0:T(8,128)(2,1)}, bf16[8,64,2048]{2,1,0:T(8,128)(2,1)}, u32[]{:S(2)}, u32[]{:S(2)}) %collective-permute-start.1) | collective-permute-done | bytes 2097184 | tf_op jit(solution)/shard_map/ppermute | solution.py:88
  576.9 1097.3 %while.11 = (s32[]{:T(128)}, f32[64,2,128]{2,1,0:T(2,128)S(1)}, pred[64]{0:T(512)(128)(4,1)S(1)}, bf16[8,256,2048]{1,2,0:T(8,128)(2,1)}, s32[8]{0:T(128)S(1)}, /...) while((s32[]{:T(128)}, f32[64,2,128]{2,1,0:T(2,128)S(1)}, ...), condition=%wide.region_9.10_spmd.clone, body=%wide.region_4.9_spmd.clone.sunk | while | flops 1011778432 | bytes 19286676 | solution.py:141
  578.2 15.9 conditional.3
  595.4 15.9 conditional.3
  612.5 15.9 conditional.3
  629.7 15.9 conditional.3
  646.8 15.9 conditional.3
  663.9 15.9 conditional.3
  681.1 15.9 conditional.3
  698.2 15.9 conditional.3
  715.4 15.9 conditional.3
  732.5 15.9 conditional.3
  749.7 15.9 conditional.3
  766.8 15.9 conditional.3
  784.0 15.9 conditional.3
  801.1 15.9 conditional.3
  818.3 15.9 conditional.3
  835.4 15.9 conditional.3
  852.5 15.9 conditional.3
  938.3 15.9 conditional.3
  955.4 15.9 conditional.3
  1058.3 15.9 conditional.3
  1161.2 15.9 conditional.3
  1264.0 15.9 conditional.3
  1281.2 15.9 conditional.3
  1384.0 15.9 conditional.3
  1486.9 15.9 conditional.3
  1589.8 15.9 conditional.3
  1606.9 15.9 conditional.3
  (1517 shorter events, 1590.4 us)
Async XLA Ops:
  16.3 48.2 %copy-start.7 = (bf16[8,64,1024]{2,1,0:T(8,128)(2,1)S(1)}, bf16[8,64,1024]{2,1,0:T(8,128)(2,1)}, u32[]{:S(2)}) copy-start(bf16[8,64,1024]{2,1,0:T(8,128)(2,1)} %param.17) | copy-start | bytes 3145732
  16.3 547.1 %all-to-all-start = ((bf16[4,16,128,1024]{3,2,1,0:T(8,128)(2,1)}), bf16[4,16,128,1024]{3,2,1,0:T(8,128)(2,1)}, u32[]{:S(2)}, u32[]{:S(2)}) async-start(bf16[4,16,128,1024]{3,2,1,0:T(8,128)(2,1)} %bitcast.114), calls=%async_computation | async-start | bytes 33554432 | tf_op jit(solution)/shard_map/all_to_all | solution.py:66
  23.5 41.1 %all-gather.4.cloned.1.call-start = ((), (), s32[]{:S(2)}) async-start(), calls=%async_computation.1 | async-start | bytes 4718592 | tf_op jit(solution)/shard_map/all_gather | solution.py:35
  24.2 464.3 %all-gather.6.cloned.1.call-start = ((), (), s32[]{:S(2)}) async-start(), calls=%async_computation.2 | async-start | bytes 4718592 | tf_op jit(solution)/shard_map/all_gather | solution.py:36
  24.9 552.0 %all-gather.8.cloned.1.call-start = ((), (), s32[]{:S(2)}) async-start(), calls=%async_computation.3 | async-start | bytes 2359296 | tf_op jit(solution)/shard_map/all_gather | solution.py:37
  64.6 409.6 %copy-start.6 = (s32[8]{0:T(128)S(1)}, s32[8]{0:T(128)}, u32[]{:S(2)}) copy-start(s32[8]{0:T(128)} %param.19) | copy-start | bytes 100
  64.6 410.1 %copy-start.3 = (bf16[128,256]{1,0:T(8,128)(2,1)S(1)}, bf16[128,256]{1,0:T(8,128)(2,1)}, u32[]{:S(2)}) copy-start(bf16[128,256]{1,0:T(8,128)(2,1)} %param.27) | copy-start | bytes 196612
  71.0 270.9 %collective-permute-start = (bf16[8,64,2048]{2,1,0:T(8,128)(2,1)}, bf16[8,64,2048]{2,1,0:T(8,128)(2,1)}, u32[]{:S(2)}, u32[]{:S(2)}) collective-permute-start(bf16[8,64,2048]{2,1,0:T(8,128)(2,1)} %bitcast.13), channel_id=1, source_target_pairs={{0,1},{1,2},{2,3},{3,0},{4,5},{5,6},{6,7},{7,4},{8,9},{9,10},{10,1... | collective-permute-start | bytes 6291464 | tf_op jit(solution)/shard_map/ppermute | solution.py:88
  72.2 420.4 %collective-permute-start.2 = (bf16[8,64,2048]{2,1,0:T(8,128)(2,1)}, bf16[8,64,2048]{2,1,0:T(8,128)(2,1)}, u32[]{:S(2)}, u32[]{:S(2)}) collective-permute-start(bf16[8,64,2048]{2,1,0:T(8,128)(2,1)} %bitcast.13), channel_id=1, source_target_pairs={{1,0},{2,1},{3,2},{0,3},{5,4},{6,5},{7,6},{4,7},{9,8},{10,9},{11,1... | collective-permute-start | bytes 6291464 | tf_op jit(solution)/shard_map/ppermute | solution.py:90
  341.8 175.9 %collective-permute-start.1 = (bf16[8,64,2048]{2,1,0:T(8,128)(2,1)}, bf16[8,64,2048]{2,1,0:T(8,128)(2,1)}, u32[]{:S(2)}, u32[]{:S(2)}) collective-permute-start(bf16[8,64,2048]{2,1,0:T(8,128)(2,1)} %collective-permute-done), channel_id=1, source_target_pairs={{0,1},{1,2},{2,3},{3,0},{4,5},{5,6},{6,7},{7,4},{8,9},{9,10},{10,1... | collective-permute-start | bytes 6291464 | tf_op jit(solution)/shard_map/ppermute | solution.py:88
  563.5 13.5 copy-start.5
  563.5 13.5 copy-start.8
  563.5 13.5 copy-start.9
  576.9 1097.4 %copy-start.4 = (s32[8,1024]{1,0:T(8,128)S(1)}, s32[8,1024]{1,0:T(8,128)}, u32[]{:S(2)}) copy-start(s32[8,1024]{1,0:T(8,128)} %param.23) | copy-start | bytes 98308
  600.2 4.7 copy-start.2
  617.3 4.7 copy-start.2
  668.8 4.7 copy-start.2
  685.9 4.7 copy-start.2
  703.1 4.7 copy-start.2
  720.2 4.7 copy-start.2
  737.4 4.7 copy-start.2
  771.7 4.7 copy-start.2
  788.8 4.7 copy-start.2
  805.9 4.7 copy-start.2
  823.1 4.7 copy-start.2
  840.2 4.7 copy-start.2
  874.5 4.7 copy-start.2
  891.7 4.7 copy-start.2
  908.8 4.7 copy-start.2
  926.0 4.7 copy-start.2
  943.1 4.7 copy-start.2
  994.5 4.7 copy-start.2
  (48 other events, 221.9 us)
Sparse Core Ops, SparseCore 0:
  26.1 38.3 all-gather.3
  66.4 36.5 all-gather.5
  474.1 29.4 all-gather.7
